TPU v7x, 256 devices: a whole 4x4x8 slice. The times are simulated.
256 devices in a mesh: row: 32 (over z_hi, y, core), col: 8 (over z_lo, x).
Axes of the slice: x: 4, y: 4, z: 8 (z_hi: 4, z_lo: 2; z = z_hi * 2 + z_lo), core: 2. Of those that a mesh axis runs over, the one named last changes fastest.
Arguments:
- left: float32 [128, 16384], P('col', 'row'), may hold values from -12 to 12
- right: float32 [128, 16384], P('row', 'col'), may hold values from -12 to 12
- w_out: float32 [1024, 128], replicated, may hold values from -0.1875 to 0.1875
- b_out: float32 [128], replicated, may hold values from -3 to 3
- pair_grad: float32 [512, 512, 128], P('row', 'col'), may hold values from -6 to 6
Outputs:
- pair_out: float32 [512, 512, 128], P('row', 'col')
- grad_left: float32 [128, 16384], P('col', 'row')
- grad_right: float32 [128, 16384], P('row', 'col')
- grad_weight: float32 [1024, 128], replicated
- grad_bias: float32 [128], replicated
All inputs are finite; a program needn't handle non-finite values.
Results may differ from a plain program's by a relative error of at most 0.0001.
Values sent between devices are 32-bit elements; how exact they have to be, the bound alone decides.
No kernel may reach another device: no remote copies, remote signals or barrier semaphores. Data moves between devices by JAX's collectives and lax.ppermute only.
A program may use at most 128 MiB of HBM per device.

v0:
```python
import jax
import jax.numpy as jnp
from jax import lax
from jax.sharding import PartitionSpec as P

C = 32
Z = 128
S = 128


def body(left, right, w_out, b_out, pair_grad):
    highest = lax.Precision.HIGHEST
    tile_rows = left.shape[1] // C
    tile_cols = right.shape[1] // C
    residues = tile_rows * lax.axis_size("row")
    weight_cube = w_out.reshape(C, C, Z)
    contract_rows = (((0,), (0,)), ((), ()))
    contract_cols = (((1,), (1,)), ((), ()))
    left_all = lax.all_gather(left, "col", axis=0, tiled=True)
    right_all = lax.all_gather(right, "row", axis=0, tiled=True)
    outer = (
        lax.dot_general(
            left_all,
            right_all,
            contract_rows,
            precision=highest,
            preferred_element_type=jnp.float32,
        )
        / S
    )
    outer_split = outer.reshape(tile_rows, C, tile_cols, C)
    pair_out = jnp.einsum("icje,cez->ijz", outer_split, weight_cube, precision=highest) + b_out
    grad_outer = jnp.einsum("ijz,cez->icje", pair_grad, weight_cube, precision=highest)
    grad_outer = grad_outer.reshape(tile_rows * C, tile_cols * C)
    grad_left = lax.psum_scatter(
        lax.dot_general(
            right_all,
            grad_outer,
            contract_cols,
            precision=highest,
            preferred_element_type=jnp.float32,
        )
        / S,
        "col",
        scatter_dimension=0,
        tiled=True,
    )
    grad_right = lax.psum_scatter(
        jnp.dot(left_all, grad_outer, precision=highest) / S, "row", scatter_dimension=0, tiled=True
    )
    weight_term = jnp.einsum("icje,ijz->cez", outer_split, pair_grad, precision=highest).reshape(
        C * C, Z
    )
    bias_term = jnp.sum(pair_grad, axis=(0, 1))
    grad_weight, grad_bias = lax.psum((weight_term, bias_term), ("row", "col"))
    return (pair_out, grad_left, grad_right, grad_weight / residues, grad_bias / residues)


def solution(mesh):
    placed = (P("col", "row"), P("row", "col"), P(), P(), P("row", "col", None))
    return jax.shard_map(
        body,
        mesh=mesh,
        in_specs=placed,
        out_specs=(P("row", "col", None), P("col", "row"), P("row", "col"), P(), P()),
        check_vma=False,
    )
```

profile of v0, /device:TPU:8, one launch (start us, length us, event | category | flops | bytes accessed | tf_op | source)
XLA Modules:
  0.0 770.1 jit_solution(7213743941106208333)
XLA Ops:
  7.2 0.0 copy-start
  7.2 0.0 all-reduce.6.cloned.1.call-start
  7.2 29.5 %all_gather.6 = f32[128,512]{1,0:T(8,128)S(1)} all-gather(f32[16,512]{1,0:T(8,128)} %param.5), channel_id=1, replica_groups=mesh['row'=32,'col'=8] {'col'}, dimensions={0}, use_global_device_ids=true | all-gather | bytes 294912 | tf_op jit(solution)/shard_map/all_gather | solution.py:19
  36.8 0.0 copy-done
  36.8 9.8 %convolution_bitcast_fusion = f32[16,32,64,32]{2,3,0,1:T(8,128)} fusion(f32[32,32,128,1]{2,1,3,0:T(8,128)S(1)} %bitcast.42, f32[16,64,128]{2,1,0:T(8,128)} %param.9), kind=kOutput, calls=%fused_computation.1 | convolution fusion | flops 1610612736 | bytes 5242880 | tf_op jit(solution)/shard_map/ijz,cez->icje/dot_general | solution.py:33
  46.6 12.3 %copy.21 = f32[16,32,64,32]{3,2,1,0:T(8,128)} copy(f32[16,32,64,32]{2,3,0,1:T(8,128)} %convolution_bitcast_fusion) | data formatting | bytes 8388608 | tf_op jit(solution)/shard_map/ijz,cez->icje/transpose | solution.py:33
  58.9 0.0 copy-start.1
  58.9 0.0 copy-start.3
  58.9 13.5 %reshape.24 = f32[512,2048]{1,0:T(8,128)} reshape(f32[16,32,64,32]{3,2,1,0:T(8,128)} %copy.21) | data formatting | bytes 8388608 | tf_op jit(solution)/shard_map/reshape | solution.py:34
  72.4 9.9 %fusion = f32[128,2048]{0,1:T(8,128)} fusion(f32[512,2048]{1,0:T(8,128)} %reshape.24, f32[128,512]{1,0:T(8,128)S(1)} %all_gather.6), kind=kOutput, calls=%fused_computation.3 | convolution fusion | flops 1610874880 | bytes 5505024 | tf_op jit(solution)/shard_map/dot_general | solution.py:49
  82.2 0.0 all-reduce.6.cloned.1.call-update
  82.3 0.0 all-gather.3.cloned.1.call-start
  82.3 0.7 all-gather.3.cloned.1.call-update
  83.0 0.2 all-reduce.4.cloned.1.call-start
  83.2 0.0 copy-done.1
  83.3 0.2 reduce_sum.9
  83.4 0.0 copy-done.3
  83.4 0.6 dynamic-slice
  84.7 77.5 %psum.15 = f32[128]{0:T(128)S(1)} all-reduce(f32[128]{0:T(128)S(1)} %reduce_sum.9), channel_id=1, replica_groups=mesh['row'=32,'col'=8] {'row','col'}, use_global_device_ids=true, to_apply=%region_4.0 | all-reduce | flops 128 | bytes 1024 | tf_op jit(solution)/shard_map/psum | solution.py:55
  162.1 0.5 broadcast_multiply_fusion.1
  162.6 205.9 %all-reduce.6.cloned.1.call-done = f32[128,2048]{0,1:T(8,128)} async-done(((f32[128,2048]{0,1:T(8,128)}), f32[128,2048]{0,1:T(8,128)}) %all-reduce.6.cloned.1.call-update) | async-done | bytes 1048592
  368.6 1.6 constant_dynamic-slice_fusion
  370.1 0.9 copy.25
  371.1 55.6 %all-gather.3.cloned.1.call-done = f32[32,4,2048]{2,1,0:T(4,128)} async-done(((f32[1,4,2048]{2,1,0:T(4,128)}), f32[32,4,2048]{2,1,0:T(4,128)}) %all-gather.3.cloned.1.call-update) | async-done | bytes 1048592 | tf_op jit(solution)/shard_map/all_gather | solution.py:20
  426.7 1.6 reshape.26
  428.3 5.0 convolution_multiply_fusion
  433.3 11.4 %reshape.22 = f32[16,32,64,32]{3,2,1,0:T(8,128)} reshape(f32[512,2048]{1,0:T(8,128)} %convolution_multiply_fusion) | data formatting | bytes 8388608 | tf_op jit(solution)/shard_map/reshape | solution.py:31
  444.7 12.7 %copy.33 = f32[32,32,16,64]{3,1,0,2:T(8,128)} copy(f32[32,32,16,64]{1,3,0,2:T(8,128)} %bitcast.44) | data formatting | bytes 8388608 | tf_op jit(solution)/shard_map/icje,ijz->cez/dot_general | solution.py:51
  457.4 0.0 copy-start.2
  457.4 9.9 %convolution_bitcast_fusion.2 = f32[1024,128]{1,0:T(8,128)} fusion(f32[1024,16,64]{2,0,1:T(8,128)} %bitcast.45, f32[16,64,128]{2,1,0:T(8,128)S(1)} %copy-done.1), kind=kOutput, calls=%fused_computation.5 | convolution fusion | flops 1610612736 | bytes 5242880 | tf_op jit(solution)/shard_map/icje,ijz->cez/dot_general | solution.py:51
  467.3 0.0 all-reduce.4.cloned.1.call-update
  467.3 0.3 reduce-scatter.5.cloned.1.call-start
  467.6 5.2 fusion.2
  472.8 0.8 copy.29
  473.7 0.0 reduce-scatter.5.cloned.1.call-update
  473.7 0.0 copy-done.2
  473.7 17.6 %fusion.1 = f32[16,64,128]{2,1,0:T(8,128)} fusion(f32[16,32,64,32]{3,2,1,0:T(8,128)} %reshape.22, f32[32,32,128,1]{2,1,0,3:T(8,128)S(1)} %bitcast.43, f32[128]{0:T(128)S(1)} %copy-done.2), kind=kOutput, calls=%fused_computation.6 | convolution fusion | flops 1610743808 | bytes 5243392 | tf_op jit(solution)/shard_map/icje,cez->ijz/dot_general | solution.py:32
  491.3 230.2 %all-reduce.4.cloned.1.call-done = f32[1024,128]{1,0:T(8,128)} async-done(((f32[1024,128]{1,0:T(8,128)}), f32[1024,128]{1,0:T(8,128)}) %all-reduce.4.cloned.1.call-update) | async-done | bytes 524304 | tf_op jit(solution)/shard_map/psum | solution.py:55
  721.5 1.9 broadcast_multiply_fusion
  723.4 40.2 %reduce-scatter.5.cloned.1.call-done = f32[16,512]{1,0:T(8,128)} async-done(((f32[128,512]{1,0:T(8,128)}), f32[16,512]{1,0:T(8,128)}) %reduce-scatter.5.cloned.1.call-update) | async-done | bytes 32784
Async XLA Ops:
  7.2 29.6 %copy-start = (f32[1024,128]{1,0:T(8,128)S(1)}, f32[1024,128]{1,0:T(8,128)}, u32[]{:S(2)}) copy-start(f32[1024,128]{1,0:T(8,128)} %param.7) | copy-start | bytes 1572868
  7.2 361.4 %all-reduce.6.cloned.1.call-start = ((), (), s32[]{:S(2)}) async-start(), calls=%async_computation.4 | async-start | bytes 2097152
  58.9 24.3 %copy-start.1 = (f32[16,64,128]{2,1,0:T(8,128)S(1)}, f32[16,64,128]{2,1,0:T(8,128)}, u32[]{:S(2)}) copy-start(f32[16,64,128]{2,1,0:T(8,128)} %param.9) | copy-start | bytes 1572868
  58.9 24.5 %copy-start.3 = (u32[256]{0:T(256)S(1)}, u32[256]{0:T(256)}, u32[]{:S(2)}) copy-start(u32[256]{0:T(256)} %constant.18) | copy-start | bytes 3076
  82.3 344.4 %all-gather.3.cloned.1.call-start = ((), (), s32[]{:S(2)}) async-start(), calls=%async_computation.2 | async-start | bytes 1081344 | tf_op jit(solution)/shard_map/all_gather | solution.py:20
  83.0 638.5 %all-reduce.4.cloned.1.call-start = ((), (), s32[]{:S(2)}) async-start(), calls=%async_computation.1 | async-start | bytes 1048576 | tf_op jit(solution)/shard_map/psum | solution.py:55
  457.4 16.3 %copy-start.2 = (f32[128]{0:T(128)S(1)}, f32[128]{0:T(128)}, u32[]{:S(2)}) copy-start(f32[128]{0:T(128)} %param.8) | copy-start | bytes 1540
  467.3 296.3 %reduce-scatter.5.cloned.1.call-start = ((), (), s32[]{:S(2)}) async-start(), calls=%async_computation.3 | async-start | bytes 294912
Sparse Core Ops, SparseCore 0:
  82.4 286.1 all-reduce.5
  371.1 55.5 all-gather.2
  467.4 254.0 all-reduce.3
  724.4 39.1 reduce-scatter.4
where the time goes:
time: 771 us; the launch traced here: 770 us
  waiting for transfers between devices  533 us (69%)
  blocking collectives  107 us (14%)
  matrix products  57.4 us (7%)
  local copies, waits for them, and re-layouts  55.4 us (7%)
  between operations  14.5 us (2%)
    unnamed x6, waiting for transfers between devices  247 us
    psum x1, waiting for transfers between devices, body(): grad_weight, grad_bias = lax.psum((weight_term, bias_term), ('row', 'col'))  230 us
    psum x1, blocking collectives, body(): grad_weight, grad_bias = lax.psum((weight_term, bias_term), ('row', 'col'))  77.5 us
    all_gather x1, waiting for transfers between devices, body(): right_all = lax.all_gather(right, 'row', axis=0, tiled=True)  55.6 us
    all_gather x1, blocking collectives, body(): left_all = lax.all_gather(left, 'col', axis=0, tiled=True)  29.5 us
    dot_general x1, matrix products, body(): jnp.einsum('icje,cez->ijz', outer_split, weight_cube, precision=highest)  17.6 us
  transfers between devices with their start and end apart: 4, of which 4 were waited for; matrix products, arithmetic and copies ran while one was open for 4% of the time, Pallas kernels for 0%

commit v1 on v0

--- a/solution.py
+++ b/solution.py
@@ -6,6 +6,11 @@
 C = 32
 Z = 128
 S = 128
+
+
+def axis_by_axis(x, axis_one, axis_two):
+    partial = lax.psum(x, axis_one)
+    return lax.psum(partial, axis_two)
 
 
 def body(left, right, w_out, b_out, pair_grad):
@@ -52,7 +57,7 @@
         C * C, Z
     )
     bias_term = jnp.sum(pair_grad, axis=(0, 1))
-    grad_weight, grad_bias = lax.psum((weight_term, bias_term), ("row", "col"))
+    grad_weight, grad_bias = axis_by_axis((weight_term, bias_term), "col", "row")
     return (pair_out, grad_left, grad_right, grad_weight / residues, grad_bias / residues)
 
 

time: 771 us -> 528 us (0.68)
  waiting for transfers between devices: 533 us -> 286 us
    psum x1, waiting for transfers between devices: 230 us -> 34.3 us  [axis_by_axis(): partial = lax.psum(x, axis_one)]
    all_gather x1, waiting for transfers between devices: 55.6 us -> 26.8 us  [body(): right_all = lax.all_gather(right, 'row', axis=0, tiled=True)]
    unnamed x6, waiting for transfers between devices: 247 us -> 225 us
    psum x1 -> x2, blocking collectives: 77.5 us -> 82.1 us  [the longest x1 64.5 us: axis_by_axis(): return lax.psum(partial, axis_two)]
  transfers between devices with their start and end apart: 4 -> 4, of which waited for: 4 -> 4; matrix products, arithmetic and copies ran while one was open for 4% -> 14% of each run, Pallas kernels for 0% -> 0%
where the time goes in v1:
time: 528 us; the launch traced here: 527 us
  waiting for transfers between devices  286 us (54%)
  blocking collectives  111 us (21%)
  matrix products  56.7 us (11%)
  local copies, waits for them, and re-layouts  55.5 us (11%)
  between operations  14.5 us (3%)
    unnamed x6, waiting for transfers between devices  225 us
    psum x1, blocking collectives, axis_by_axis(): return lax.psum(partial, axis_two)  64.5 us
    psum x1, waiting for transfers between devices, axis_by_axis(): partial = lax.psum(x, axis_one)  34.3 us
    all_gather x1, blocking collectives, body(): left_all = lax.all_gather(left, 'col', axis=0, tiled=True)  29.4 us
    all_gather x1, waiting for transfers between devices, body(): right_all = lax.all_gather(right, 'row', axis=0, tiled=True)  26.8 us
    dot_general x1, matrix products, body(): jnp.einsum('icje,cez->ijz', outer_split, weight_cube, precision=highest)  17.6 us
    psum x1, blocking collectives, axis_by_axis(): partial = lax.psum(x, axis_one)  17.5 us
    reshape x1, local copies, waits for them, and re-layouts, body(): grad_outer = grad_outer.reshape(tile_rows * C, tile_cols * C)  13.4 us
  transfers between devices with their start and end apart: 4, of which 4 were waited for; matrix products, arithmetic and copies ran while one was open for 14% of the time, Pallas kernels for 0%

profile of v1, /device:TPU:8, one launch (start us, length us, event | category | flops | bytes accessed | tf_op | source)
XLA Modules:
  0.0 526.8 jit_solution(9706006411387811234)
XLA Ops:
  7.2 0.0 copy-start
  7.2 0.0 all-gather.3.cloned.1.call-start
  7.2 0.7 all-gather.3.cloned.1.call-update
  7.9 0.0 all-reduce.5.cloned.1.call-start
  8.0 29.4 %all_gather.6 = f32[128,512]{1,0:T(8,128)S(1)} all-gather(f32[16,512]{1,0:T(8,128)} %param.5), channel_id=1, replica_groups=mesh['row'=32,'col'=8] {'col'}, dimensions={0}, use_global_device_ids=true | all-gather | bytes 294912 | tf_op jit(solution)/shard_map/all_gather | solution.py:24
  37.4 26.8 %all-gather.3.cloned.1.call-done = f32[32,4,2048]{2,1,0:T(4,128)} async-done(((f32[1,4,2048]{2,1,0:T(4,128)}), f32[32,4,2048]{2,1,0:T(4,128)}) %all-gather.3.cloned.1.call-update) | async-done | bytes 1048592 | tf_op jit(solution)/shard_map/all_gather | solution.py:25
  64.2 1.6 reshape.26
  65.8 5.1 convolution_multiply_fusion
  70.9 11.4 %reshape.22 = f32[16,32,64,32]{3,2,1,0:T(8,128)} reshape(f32[512,2048]{1,0:T(8,128)} %convolution_multiply_fusion) | data formatting | bytes 8388608 | tf_op jit(solution)/shard_map/reshape | solution.py:36
  82.3 0.0 copy-start.1
  82.3 12.8 %copy.33 = f32[32,32,16,64]{3,1,0,2:T(8,128)} copy(f32[32,32,16,64]{1,3,0,2:T(8,128)} %bitcast.44) | data formatting | bytes 8388608 | tf_op jit(solution)/shard_map/icje,ijz->cez/dot_general | solution.py:56
  95.1 0.0 copy-done.1
  95.1 9.9 %convolution_bitcast_fusion.2 = f32[1024,128]{1,0:T(8,128)} fusion(f32[1024,16,64]{2,0,1:T(8,128)} %bitcast.45, f32[16,64,128]{2,1,0:T(8,128)S(1)} %copy-done.1), kind=kOutput, calls=%fused_computation.5 | convolution fusion | flops 1610612736 | bytes 5242880 | tf_op jit(solution)/shard_map/icje,ijz->cez/dot_general | solution.py:56
  104.9 0.0 all-reduce.5.cloned.1.call-update
  105.0 0.2 all-reduce.7.cloned.1.call-start
  105.2 0.0 copy-done
  105.2 9.0 %convolution_bitcast_fusion = f32[16,32,64,32]{2,3,0,1:T(8,128)} fusion(f32[32,32,128,1]{2,1,3,0:T(8,128)S(1)} %bitcast.43, f32[16,64,128]{2,1,0:T(8,128)S(1)} %copy-done.1), kind=kOutput, calls=%fused_computation.1 | convolution fusion | flops 1610612736 | bytes 5242880 | tf_op jit(solution)/shard_map/ijz,cez->icje/dot_general | solution.py:38
  114.2 12.3 %copy.21 = f32[16,32,64,32]{3,2,1,0:T(8,128)} copy(f32[16,32,64,32]{2,3,0,1:T(8,128)} %convolution_bitcast_fusion) | data formatting | bytes 8388608 | tf_op jit(solution)/shard_map/ijz,cez->icje/transpose | solution.py:38
  126.5 0.0 copy-start.3
  126.5 13.4 %reshape.24 = f32[512,2048]{1,0:T(8,128)} reshape(f32[16,32,64,32]{3,2,1,0:T(8,128)} %copy.21) | data formatting | bytes 8388608 | tf_op jit(solution)/shard_map/reshape | solution.py:39
  140.0 0.0 copy-start.2
  140.0 9.9 %fusion = f32[128,2048]{0,1:T(8,128)} fusion(f32[512,2048]{1,0:T(8,128)} %reshape.24, f32[128,512]{1,0:T(8,128)S(1)} %all_gather.6), kind=kOutput, calls=%fused_computation.3 | convolution fusion | flops 1610874880 | bytes 5505024 | tf_op jit(solution)/shard_map/dot_general | solution.py:54
  149.9 34.3 %all-reduce.5.cloned.1.call-done = f32[1024,128]{1,0:T(8,128)} async-done(((f32[1024,128]{1,0:T(8,128)}), f32[1024,128]{1,0:T(8,128)}) %all-reduce.5.cloned.1.call-update) | async-done | bytes 524304 | tf_op jit(solution)/shard_map/psum | solution.py:12
  184.2 0.0 all-reduce.7.cloned.1.call-update
  184.2 0.0 reduce-scatter.5.cloned.1.call-start
  184.3 0.2 reduce_sum.9
  184.4 0.0 copy-done.3
  184.4 0.6 dynamic-slice
  185.7 17.5 %psum.30 = f32[128]{0:T(128)S(1)} all-reduce(f32[128]{0:T(128)S(1)} %reduce_sum.9), channel_id=1, replica_groups=mesh['row'=32,'col'=8] {'col'}, use_global_device_ids=true, to_apply=%region_5.0 | all-reduce | flops 128 | bytes 1024 | tf_op jit(solution)/shard_map/psum | solution.py:12
  203.2 64.5 %psum.31 = f32[128]{0:T(128)S(1)} all-reduce(f32[128]{0:T(128)S(1)} %psum.30), channel_id=1, replica_groups=mesh['row'=32,'col'=8] {'row'}, use_global_device_ids=true, to_apply=%region_6.0 | all-reduce | flops 128 | bytes 1024 | tf_op jit(solution)/shard_map/psum | solution.py:13
  267.7 0.5 broadcast_multiply_fusion.1
  268.3 5.2 fusion.2
  273.5 0.8 copy.29
  274.3 0.0 reduce-scatter.5.cloned.1.call-update
  274.3 0.0 copy-done.2
  274.4 17.6 %fusion.1 = f32[16,64,128]{2,1,0:T(8,128)} fusion(f32[16,32,64,32]{3,2,1,0:T(8,128)} %reshape.22, f32[32,32,128,1]{2,1,0,3:T(8,128)S(1)} %bitcast.42, f32[128]{0:T(128)S(1)} %copy-done.2), kind=kOutput, calls=%fused_computation.6 | convolution fusion | flops 1610743808 | bytes 5243392 | tf_op jit(solution)/shard_map/icje,cez->ijz/dot_general | solution.py:37
  291.9 180.5 %all-reduce.7.cloned.1.call-done = (f32[128,2048]{0,1:T(8,128)}, f32[1024,128]{1,0:T(8,128)}) async-done(((f32[128,2048]{0,1:T(8,128)}, f32[1024,128]{1,0:T(8,128)}), (f32[128,2048]{0,1:T(8,128)}, f32[1024,128]{1,0:T(8,128)})) %all-reduce.7.cloned.1.call-update) | async-done | bytes 1572880
  472.4 1.6 constant_dynamic-slice_fusion
  473.9 0.9 copy.25
  474.9 1.9 broadcast_multiply_fusion
  476.8 43.5 %reduce-scatter.5.cloned.1.call-done = f32[16,512]{1,0:T(8,128)} async-done(((f32[128,512]{1,0:T(8,128)}), f32[16,512]{1,0:T(8,128)}) %reduce-scatter.5.cloned.1.call-update) | async-done | bytes 32784
Async XLA Ops:
  7.2 98.0 %copy-start = (f32[1024,128]{1,0:T(8,128)S(1)}, f32[1024,128]{1,0:T(8,128)}, u32[]{:S(2)}) copy-start(f32[1024,128]{1,0:T(8,128)} %param.7) | copy-start | bytes 1572868
  7.2 57.0 %all-gather.3.cloned.1.call-start = ((), (), s32[]{:S(2)}) async-start(), calls=%async_computation.2 | async-start | bytes 1081344 | tf_op jit(solution)/shard_map/all_gather | solution.py:25
  7.9 176.3 %all-reduce.5.cloned.1.call-start = ((), (), s32[]{:S(2)}) async-start(), calls=%async_computation.1 | async-start | bytes 1048576 | tf_op jit(solution)/shard_map/psum | solution.py:12
  82.3 12.8 %copy-start.1 = (f32[16,64,128]{2,1,0:T(8,128)S(1)}, f32[16,64,128]{2,1,0:T(8,128)}, u32[]{:S(2)}) copy-start(f32[16,64,128]{2,1,0:T(8,128)} %param.9) | copy-start | bytes 1572868
  105.0 367.4 %all-reduce.7.cloned.1.call-start = ((), (), s32[]{:S(2)}) async-start(), calls=%async_computation.4 | async-start | bytes 3145728
  126.5 57.9 %copy-start.3 = (u32[256]{0:T(256)S(1)}, u32[256]{0:T(256)}, u32[]{:S(2)}) copy-start(u32[256]{0:T(256)} %constant.18) | copy-start | bytes 3076
  140.0 134.4 %copy-start.2 = (f32[128]{0:T(128)S(1)}, f32[128]{0:T(128)}, u32[]{:S(2)}) copy-start(f32[128]{0:T(128)} %param.8) | copy-start | bytes 1540
  184.2 336.0 %reduce-scatter.5.cloned.1.call-start = ((), (), s32[]{:S(2)}) async-start(), calls=%async_computation.3 | async-start | bytes 294912
Sparse Core Ops, SparseCore 0:
  10.5 53.5 all-gather.2
  105.1 79.0 all-reduce.4
  186.9 285.4 all-reduce.6
  475.3 44.8 reduce-scatter.4
